TPU v7x, 32 devices: a whole 2x2x4 slice. The times are simulated.
32 devices in a mesh: batch: 4 (over z), expert: 8 (over y, x, core).
Axes of the slice: x: 2, y: 2, z: 4, core: 2. Of those that a mesh axis runs over, the one named last changes fastest.
Arguments:
- tokens: bfloat16 [8192, 1024], P(('batch', 'expert')), may hold values from -6 to 6
- doc_ends: int32 [32, 4], P(('batch', 'expert')), may hold values from 8 to 256, as said below
- routes: int32 [8192, 1], P(('batch', 'expert')), may hold values from 0 to 7, as said below
- w_query: bfloat16 [1024, 1024], replicated, may hold values from -0.1875 to 0.1875
- w_key: bfloat16 [1024, 1024], replicated, may hold values from -0.1875 to 0.1875
- w_value: bfloat16 [1024, 1024], replicated, may hold values from -0.1875 to 0.1875
- w_output: bfloat16 [1024, 1024], replicated, may hold values from -0.5 to 0.5
- attn_gain: float32 [1024], replicated, may hold values from 0.1 to 1.9
- centroids: float32 [8, 1024], replicated, may hold values from -0.15 to 0.15
- up_first: bfloat16 [8, 1024, 4096], P('expert'), may hold values from -0.1875 to 0.1875
- down_first: bfloat16 [8, 4096, 1024], P('expert'), may hold values from -0.09375 to 0.09375
- gain_first: float32 [8, 1024], P('expert'), may hold values from 0.1 to 1.9
- up_second: bfloat16 [8, 1024, 4096], P('expert'), may hold values from -0.1875 to 0.1875
- down_second: bfloat16 [8, 4096, 1024], P('expert'), may hold values from -0.09375 to 0.09375
- gain_second: float32 [8, 1024], P('expert'), may hold values from 0.1 to 1.9
- cotangent: bfloat16 [8192, 1024], P(('batch', 'expert')), may hold values from -6 to 6
Outputs:
- block_out: bfloat16 [8192, 1024], P(('batch', 'expert'))
- grad_tokens: float32 [8192, 1024], P(('batch', 'expert'))
- grad_query: float32 [1024, 1024], P(('batch', 'expert'))
- grad_key: float32 [1024, 1024], P(('batch', 'expert'))
- grad_value: float32 [1024, 1024], P(('batch', 'expert'))
- grad_output: float32 [1024, 1024], P(('batch', 'expert'))
- grad_attn_gain: float32 [1024], replicated
- grad_centroids: float32 [8, 1024], replicated
- grad_up_first: float32 [8, 1024, 4096], P('expert', None, 'batch')
- grad_down_first: float32 [8, 4096, 1024], P('expert', 'batch')
- grad_gain_first: float32 [8, 1024], P('expert', 'batch')
- grad_up_second: float32 [8, 1024, 4096], P('expert', None, 'batch')
- grad_down_second: float32 [8, 4096, 1024], P('expert', 'batch')
- grad_gain_second: float32 [8, 1024], P('expert', 'batch')
Inputs may be any that keep to these rules, and one draw needn't show every extreme that they name: `routes`: each device's 256 slots send at most 44 to any one expert; one expert, chosen by the draw, receives exactly 44 slots from every device. `doc_ends`: each row holds 4 nondecreasing document ends of one device's slots; slots at or past the last end are padding; a document may be empty; on some device the last end is 256, and on some device the first end is 8.
All inputs are finite; a program needn't handle non-finite values.
Results may differ from a plain program's by a relative error of at most 0.014.
Values may be sent and summed in bfloat16 or wider, within the bound.
A program may use at most 256 MiB of HBM per device.

v0:
```python
import functools
import jax, jax.numpy as jnp
from jax import lax
from jax.experimental import pallas as pl
from jax.experimental.pallas import tpu as pltpu
from jax.sharding import PartitionSpec as P


MESH = pl.DeviceIdType.MESH
BF = jnp.bfloat16
F32 = jnp.float32
GELU_A = 0.7978845608028654
GELU_B = 0.044715


def gelu_pair(v):
    square = v * v
    bent = jnp.tanh(GELU_A * v * (1.0 + GELU_B * square))
    half = 0.5 * (1.0 + bent)
    slope = half + 0.5 * v * (1.0 - bent * bent) * (GELU_A * (1.0 + 3.0 * GELU_B * square))
    return v * half, slope


def dot(a, b, dims=((1,), (0,))):
    return lax.dot_general(a, b, (dims, ((), ())), preferred_element_type=F32)


MASKED = -1e30
EPSILON = 1e-05


def split_three(value):
    high = value.astype(BF)
    rest = value - high.astype(F32)
    middle = rest.astype(BF)
    return high, middle, (rest - middle.astype(F32)).astype(BF)


def select_rows(marks, value, dims):
    return sum(dot(marks, term, dims) for term in split_three(value))


def norm_parts(stream):
    average = jnp.mean(stream, axis=-1, keepdims=True)
    centred = stream - average
    variance = jnp.mean(centred * centred, axis=-1, keepdims=True)
    scale = lax.rsqrt(variance + EPSILON)
    return centred * scale, scale


def norm_pull(grad, stream, gain):
    unit, scale = norm_parts(stream)
    inner = grad * gain
    mean_inner = jnp.mean(inner, axis=-1, keepdims=True)
    mean_product = jnp.mean(inner * unit, axis=-1, keepdims=True)
    return scale * (inner - mean_inner - unit * mean_product), jnp.sum(grad * unit, axis=0, keepdims=True)


def route_marks(routes_row, experts, slots):
    count = routes_row.shape[1]
    ids = lax.broadcasted_iota(jnp.int32, (experts, count), 0)
    chosen = (ids == routes_row).astype(F32)
    earlier = lax.broadcasted_iota(jnp.int32, (count, count), 0) <= lax.broadcasted_iota(jnp.int32, (count, count), 1)
    running = dot(chosen.astype(BF), earlier.astype(F32).astype(BF))
    rank = jnp.sum(running * chosen, axis=0, keepdims=True) - 1.0
    place = routes_row * slots + rank.astype(jnp.int32)
    rows = lax.broadcasted_iota(jnp.int32, (experts * slots, count), 0)
    return chosen.astype(BF), (rows == place).astype(F32).astype(BF)


def allowed_pairs(ends, docs, count):
    row = lax.broadcasted_iota(jnp.int32, (count, count), 0)
    col = lax.broadcasted_iota(jnp.int32, (count, count), 1)
    row_segment = jnp.zeros((count, count), jnp.int32)
    col_segment = jnp.zeros((count, count), jnp.int32)
    for d in range(docs):
        row_segment += (row >= ends[0, d]).astype(jnp.int32)
        col_segment += (col >= ends[0, d]).astype(jnp.int32)
    return (row_segment == col_segment) & (col <= row)


def half_marks(half):
    lane = lax.broadcasted_iota(jnp.int32, (1, 128), 1)
    inside = (lane >= 64 * half) & (lane < 64 * half + 64)
    return inside.astype(F32).astype(BF)


def head_shares(query_pair, key_pair, allowed, half):
    raw = dot(query_pair * half_marks(half), key_pair, ((1,), (1,)))
    scores = jnp.where(allowed, raw * 0.125, MASKED)
    raised = jnp.exp(scores - jnp.max(scores, axis=-1, keepdims=True))
    return raised * (1.0 / jnp.sum(raised, axis=-1, keepdims=True))


def join_halves(first, second):
    lane = lax.broadcasted_iota(jnp.int32, first.shape, 1)
    return jnp.where(lane < 64, first, second)


def forward_pair(allowed, queries, keys, values, mixed, j, carry):
    cols = pl.ds(pl.multiple_of(j * 128, 128), 128)
    query_pair, key_pair, value_pair = queries[:, cols], keys[:, cols], values[:, cols]
    halves = [dot(head_shares(query_pair, key_pair, allowed, half).astype(BF), value_pair) for half in range(2)]
    mixed[:, cols] = join_halves(*halves).astype(BF)
    return carry


def enter_kernel(
    experts, slots, docs,
    ends, routes, tokens, cotangent, gain, cents, w_query, w_key, w_value, w_output,
    normed, queries, keys, values, mixed, hidden, out_rows,
    w_held, sems,
):
    copies = [
        pltpu.make_async_copy(w, w_held.at[i], sems.at[i])
        for i, w in enumerate((w_query, w_key, w_value, w_output))
    ]
    for copy in copies:
        copy.start()
    count, wide = tokens.shape
    unit, _ = norm_parts(tokens[...].astype(F32))
    normed[...] = (unit * gain[...]).astype(BF)
    for i, result in enumerate((queries, keys, values)):
        copies[i].wait()
        result[...] = dot(normed[...], w_held[i]).astype(BF)
    allowed = allowed_pairs(ends, docs, count)

    lax.fori_loop(0, wide // 128, functools.partial(forward_pair, allowed, queries, keys, values, mixed), 0)
    copies[3].wait()
    hidden[...] = tokens[...].astype(F32) + dot(mixed[...], w_held[3])
    chosen, dispatch = route_marks(routes[...], experts, slots)
    own = select_rows(chosen, cents[...], ((0,), (0,)))
    gating = jax.nn.sigmoid(jnp.sum(hidden[...] * own, axis=-1, keepdims=True))
    live = (lax.broadcasted_iota(jnp.int32, (count, 1), 0) < ends[0, docs - 1]).astype(F32)
    grad_sent = (gating * (live * cotangent[...].astype(F32))).astype(BF)
    for kind, rows in enumerate((hidden[...].astype(BF), grad_sent)):
        out_rows[kind] = dot(dispatch, rows).astype(BF).reshape(experts, slots, wide)


def enter(ends, routes_row, tokens, cotangent, gain, cents, weights, slots):
    count, wide = tokens.shape
    experts, docs = cents.shape[0], ends.shape[1]
    vmem = pl.BlockSpec(memory_space=pltpu.VMEM)
    anys = pl.BlockSpec(memory_space=pl.ANY)
    low = jax.ShapeDtypeStruct((count, wide), BF)
    return pl.pallas_call(
        functools.partial(enter_kernel, experts, slots, docs),
        out_shape=(low,) * 5 + (
            jax.ShapeDtypeStruct((count, wide), F32),
            jax.ShapeDtypeStruct((2, experts, slots, wide), BF),
        ),
        in_specs=[pl.BlockSpec(memory_space=pltpu.SMEM)] + [vmem] * 5 + [anys] * 4,
        out_specs=(vmem,) * 7,
        scratch_shapes=[pltpu.VMEM((4, wide, wide), BF), pltpu.SemaphoreType.DMA((4,))],
        compiler_params=pltpu.CompilerParams(vmem_limit_bytes=48 * 1024 * 1024),
        name="enter",
    )(ends, routes_row, tokens, cotangent, gain, cents, *weights)


def backward_pair(allowed, queries, keys, values, grad_low, grad_three, j, carry):
    cols = pl.ds(pl.multiple_of(j * 128, 128), 128)
    query_pair, key_pair, value_pair = queries[:, cols], keys[:, cols], values[:, cols]
    grad_pair = grad_low[:, cols]
    parts = []
    for half in range(2):
        shares = head_shares(query_pair, key_pair, allowed, half)
        grad_shares = dot(grad_pair * half_marks(half), value_pair, ((1,), (1,)))
        inner = jnp.sum(shares * grad_shares, axis=-1, keepdims=True)
        raw = (shares * (grad_shares - inner) * 0.125).astype(BF)
        parts.append((
            dot(raw, key_pair),
            dot(raw, query_pair, ((0,), (0,))),
            dot(shares.astype(BF), grad_pair, ((0,), (0,))),
        ))
    for i in range(3):
        grad_three[i][:, cols] = join_halves(parts[0][i], parts[1][i]).astype(BF)
    return carry


def leave_kernel(
    experts, slots, docs,
    ends, routes, tokens, cotangent, gain, cents, normed, queries, keys, values, mixed, hidden, came,
    w_query, w_key, w_value, w_output,
    block_out, grad_tokens, dense, small,
    w_held, grad_low, grad_three, normed_turned, grad_hidden, sems,
):
    copies = [
        pltpu.make_async_copy(w, w_held.at[i], sems.at[i])
        for i, w in enumerate((w_query, w_key, w_value, w_output))
    ]
    for i in (3, 0, 1, 2):
        copies[i].start()
    count, wide = tokens.shape
    chosen, dispatch = route_marks(routes[...], experts, slots)
    own = select_rows(chosen, cents[...], ((0,), (0,)))
    gating = jax.nn.sigmoid(jnp.sum(hidden[...] * own, axis=-1, keepdims=True))
    live = (lax.broadcasted_iota(jnp.int32, (count, 1), 0) < ends[0, docs - 1]).astype(F32)
    returned = dot(dispatch, came[0], ((0,), (0,)))
    block_out[...] = (live * (gating * returned + (1.0 - gating) * hidden[...])).astype(BF)
    grad_block = live * cotangent[...].astype(F32)
    grad_score = jnp.sum(grad_block * (returned - hidden[...]), axis=-1, keepdims=True) * gating * (1.0 - gating)
    grad_hidden[...] = (1.0 - gating) * grad_block + dot(dispatch, came[1], ((0,), (0,))) + grad_score * own
    small[pl.ds(8, experts), :] = select_rows(chosen, grad_score * hidden[...], ((1,), (0,)))
    grad_low[...] = grad_hidden[...].astype(BF)
    copies[3].wait()
    grad_mixed = dot(grad_low[...], w_held[3], ((1,), (1,))).astype(BF)
    dense[3] = dot(mixed[...].T, grad_low[...]).astype(BF)
    grad_low[...] = grad_mixed
    allowed = allowed_pairs(ends, docs, count)

    lax.fori_loop(
        0, wide // 128, functools.partial(
            backward_pair, allowed, queries, keys, values, grad_low, [grad_three.at[i] for i in range(3)]
        ), 0
    )
    normed_turned[...] = normed[...].T
    for i in range(3):
        dense[i] = dot(normed_turned[...], grad_three[i]).astype(BF)
    for i in range(3):
        copies[i].wait()
    grad_normed = sum(dot(grad_three[i], w_held[i], ((1,), (1,))) for i in range(3))
    pulled, grad_gain = norm_pull(grad_normed, tokens[...].astype(F32), gain[...])
    grad_tokens[...] = grad_hidden[...] + pulled
    small[pl.ds(0, 8), :] = jnp.broadcast_to(grad_gain, (8, wide))


def leave(ends, routes_row, tokens, cotangent, gain, cents, kept, came, weights, slots):
    count, wide = tokens.shape
    experts, docs = cents.shape[0], ends.shape[1]
    vmem = pl.BlockSpec(memory_space=pltpu.VMEM)
    anys = pl.BlockSpec(memory_space=pl.ANY)
    return pl.pallas_call(
        functools.partial(leave_kernel, experts, slots, docs),
        out_shape=(
            jax.ShapeDtypeStruct((count, wide), BF),
            jax.ShapeDtypeStruct((count, wide), F32),
            jax.ShapeDtypeStruct((4, wide, wide), BF),
            jax.ShapeDtypeStruct((8 + experts, wide), F32),
        ),
        in_specs=[pl.BlockSpec(memory_space=pltpu.SMEM)] + [vmem] * 12 + [anys] * 4,
        out_specs=(vmem,) * 4,
        scratch_shapes=[
            pltpu.VMEM((4, wide, wide), BF),
            pltpu.VMEM((count, wide), BF),
            pltpu.VMEM((3, count, wide), BF),
            pltpu.VMEM((wide, count), BF),
            pltpu.VMEM((count, wide), F32),
            pltpu.SemaphoreType.DMA((4,)),
        ],
        compiler_params=pltpu.CompilerParams(vmem_limit_bytes=56 * 1024 * 1024),
        name="leave",
    )(ends, routes_row, tokens, cotangent, gain, cents, *kept, came, *weights)


def pack_marks(experts, slots, capacity):
    shape = (experts * capacity, experts * slots)
    row = lax.broadcasted_iota(jnp.int32, (shape[0], 1), 0)
    block = sum((row >= s * capacity).astype(jnp.int32) for s in range(1, experts))
    column = lax.broadcasted_iota(jnp.int32, shape, 1)
    return (column == row + (slots - capacity) * block).astype(F32).astype(BF)


def chain_kernel(
    experts, slots, capacity, tiles,
    came, up_first, down_first, up_second, down_second, gain_first, gain_second,
    back, rows, gains,
    up_tile, down_tile, pre, stream, total, sems,
):
    tile = up_tile.shape[2]
    ups, downs = (up_first, up_second), (down_first, down_second)
    gain_refs = (gain_first, gain_second)

    def fetch(s, c, slot):
        cols = pl.ds(pl.multiple_of(c * tile, tile), tile)
        return (
            pltpu.make_async_copy(ups[s].at[0, :, cols], up_tile.at[slot], sems.at[0, slot]),
            pltpu.make_async_copy(downs[s].at[0, cols, :], down_tile.at[slot], sems.at[1, slot]),
        )

    order = ((0, True), (1, True), (1, False), (0, False))

    def run(phase, body):
        s = order[phase][0]

        def step(c, carry):
            slot = lax.rem(c, 2)
            for copy in fetch(s, c, slot):
                copy.wait()

            @pl.when(c + 1 < tiles)
            def _():
                for copy in fetch(s, c + 1, 1 - slot):
                    copy.start()

            if phase < 3:
                @pl.when(c + 1 == tiles)
                def _():
                    for copy in fetch(order[phase + 1][0], 0, 1 - slot):
                        copy.start()

            body(s, pl.ds(pl.multiple_of(c * tile, tile), tile), slot)
            return carry

        lax.fori_loop(0, tiles, step, 0)

    for copy in fetch(0, 0, 0):
        copy.start()
    gains[...] = jnp.zeros_like(gains)
    packing = pack_marks(experts, slots, capacity)
    stream[0] = dot(packing, came[0])
    rows[1, 1] = dot(packing, came[1]).astype(BF)

    def forward(s, cols, slot):
        made = dot(rows[0, s], up_tile[slot])
        pre[s, :, cols] = made
        mid = gelu_pair(made)[0].astype(BF)
        total[...] += dot(mid, down_tile[slot])

    def backward(s, cols, slot):
        grad_mid = dot(rows[1, s], down_tile[slot], ((1,), (1,)))
        grad_pre = (gelu_pair(pre[s, :, cols])[1] * grad_mid).astype(BF)
        total[...] += dot(grad_pre, up_tile[slot], ((1,), (1,)))

    for s in range(2):
        unit, _ = norm_parts(stream[s])
        rows[0, s] = (unit * gain_refs[s][...]).astype(BF)
        total[...] = stream[s]
        run(s, forward)
        if s == 0:
            stream[1] = total[...]
    back[0] = dot(packing, total[...].astype(BF), ((0,), (0,))).astype(BF)

    for phase, s in ((2, 1), (3, 0)):
        total[...] = jnp.zeros_like(total)
        run(phase, backward)
        pulled, grad_gain = norm_pull(total[...], stream[s], gain_refs[s][...])
        gains[pl.ds(s, 1), :] = grad_gain
        if s == 1:
            grad_stream = rows[1, 1].astype(F32) + pulled
            stream[1] = grad_stream
            rows[1, 0] = grad_stream.astype(BF)
        else:
            grad_rows = (stream[1] + pulled).astype(BF)
            back[1] = dot(packing, grad_rows, ((0,), (0,))).astype(BF)


def chain(came, up_first, down_first, up_second, down_second, gain_first, gain_second, slots, capacity):
    wide, hidden = up_first.shape[1:]
    experts = came.shape[1] // slots
    count = experts * capacity
    tile = 1024
    vmem = pl.BlockSpec(memory_space=pltpu.VMEM)
    anys = pl.BlockSpec(memory_space=pl.ANY)
    return pl.pallas_call(
        functools.partial(chain_kernel, experts, slots, capacity, hidden // tile),
        out_shape=(
            jax.ShapeDtypeStruct(came.shape, BF),
            jax.ShapeDtypeStruct((2, 2, count, wide), BF),
            jax.ShapeDtypeStruct((8, wide), F32),
        ),
        in_specs=[vmem] + [anys] * 4 + [vmem] * 2,
        out_specs=(vmem,) * 3,
        scratch_shapes=[
            pltpu.VMEM((2, wide, tile), BF),
            pltpu.VMEM((2, tile, wide), BF),
            pltpu.VMEM((2, count, hidden), F32),
            pltpu.VMEM((2, count, wide), F32),
            pltpu.VMEM((count, wide), F32),
            pltpu.SemaphoreType.DMA((2, 2)),
        ],
        compiler_params=pltpu.CompilerParams(vmem_limit_bytes=56 * 1024 * 1024),
        name="chain",
    )(came, up_first, down_first, up_second, down_second, gain_first, gain_second)


def ring_rows(rows, axis):
    count = lax.axis_size(axis)
    back = [(i, (i - 1) % count) for i in range(count)]
    held = [rows]
    for _ in range(count - 1):
        held.append(lax.ppermute(held[-1], axis, back))
    return jnp.concatenate(held, axis=0)


def weight_grads(normed_rows, grad_rows, up_proj, down_proj):
    count = lax.axis_size("batch")
    width = up_proj.shape[1] // count
    first = lax.axis_index("batch") * width
    up_part = lax.dynamic_slice_in_dim(up_proj, first, width, 1)
    down_part = lax.dynamic_slice_in_dim(down_proj, first, width, 0)
    pre_act = jnp.dot(normed_rows, up_part, preferred_element_type=jnp.float32)
    middle, gelu_pull = jax.vjp(jax.nn.gelu, pre_act)
    grad_middle = jnp.einsum("rd,fd->rf", grad_rows, down_part, preferred_element_type=jnp.float32)
    grad_pre = gelu_pull(grad_middle)[0].astype(jnp.bfloat16)
    grad_down = jnp.einsum(
        "rf,rd->fd", middle.astype(jnp.bfloat16), grad_rows, preferred_element_type=jnp.float32
    )
    grad_up = jnp.einsum("rd,rf->df", normed_rows, grad_pre, preferred_element_type=jnp.float32)
    return grad_up, grad_down


def halve(blocks, axis, bit, dim):
    count = lax.axis_size(axis)
    mine = (lax.axis_index(axis) // bit) % 2
    kept = lax.dynamic_index_in_dim(blocks, mine, dim, keepdims=False)
    sent = lax.dynamic_index_in_dim(blocks, 1 - mine, dim, keepdims=False)
    got = lax.ppermute(sent, axis, [(i, i ^ bit) for i in range(count)])
    return (kept.astype(jnp.float32) + got.astype(jnp.float32)).astype(blocks.dtype)


def scatter_sum(parts):
    experts, groups = lax.axis_size("expert"), lax.axis_size("batch")
    kinds, rows, width = parts.shape
    bits_e = experts.bit_length() - 1
    bits_b = groups.bit_length() - 1
    shape = (kinds,) + (2,) * (bits_b + bits_e) + (rows // (experts * groups), width)
    blocks = parts.reshape(shape)
    for k in range(bits_e):
        blocks = halve(blocks, "expert", 1 << k, bits_b + bits_e - k)
    for k in range(bits_b):
        blocks = halve(blocks, "batch", 1 << k, bits_b - k)
    return blocks


def all_sum(value):
    for axis in ("expert", "batch"):
        count = lax.axis_size(axis)
        bit = 1
        while bit < count:
            value = value + lax.ppermute(value, axis, [(i, i ^ bit) for i in range(count)])
            bit *= 2
    return value


def layer_kernel(
    experts, groups, slots, capacity, docs, width, tiles,
    ends, routes, tokens, cotangent, gain, cents, gain_first, gain_second,
    w_query, w_key, w_value, w_output, up_first, down_first, up_second, down_second,
    block_out, grad_tokens, dense_out, small_out, gains_out, up_one, down_one, up_two, down_two, ring_held, far_inbox,
    w_held, slopes, stream, norms, grads, cur, token_low, attention, hidden, dispatch, packing, routes_held, inbox, outbox, dense, turned, middles, up_stage,
    keep, s_got, g_got,
    w_sems, row_sem, a2a_send, a2a_recv, far_send, far_recv, route_send, route_recv, ring_send, ring_recv, dense_send, dense_recv, small_send, small_recv,
    gain_send, gain_recv, ready, out_sem,
):
    b, e = lax.axis_index("batch"), lax.axis_index("expert")
    count, wide = tokens.shape
    many = experts * capacity
    before, after = lax.rem(b + groups - 1, groups), lax.rem(b + 1, groups)
    core, x, y = lax.rem(e, 2), lax.rem(e // 2, 2), lax.rem(e // 4, 2)
    b0, b1 = lax.rem(b, 2), lax.rem(b // 2, 2)
    other = 1 - core
    to_core, to_x, to_y = (b, e + 1 - 2 * core), (b, e + 2 - 4 * x), (b, e + 4 - 8 * y)
    to_low, to_high = (b + 1 - 2 * b0, e), (b + 2 - 4 * b1, e)

    def remote(src, dst, send, recv, peer):
        return pltpu.make_async_remote_copy(
            src_ref=src, dst_ref=dst, send_sem=send, recv_sem=recv, device_id=peer, device_id_type=MESH
        )

    barrier = pltpu.get_barrier_semaphore()

    def greet(p, carry):
        peer = (b, lax.rem(e + p, experts))
        pl.semaphore_signal(barrier, inc=1, device_id=peer, device_id_type=MESH)
        return carry

    lax.fori_loop(1, experts, greet, 0)
    for peer in ((before, e), (after, e), to_high):
        pl.semaphore_signal(barrier, inc=1, device_id=peer, device_id_type=MESH)

    tile = wide
    ups, downs = (up_first, up_second), (down_first, down_second)
    gain_refs = (gain_first, gain_second)

    def fetch(s, c, slot):
        cols = pl.ds(pl.multiple_of(c * tile, tile), tile)
        return (
            pltpu.make_async_copy(ups[s].at[0, :, cols], w_held.at[slot], w_sems.at[slot]),
            pltpu.make_async_copy(downs[s].at[0, cols, :], w_held.at[2 + slot], w_sems.at[2 + slot]),
        )

    def stream_tiles(s, follow, body):
        def step(c, carry):
            slot = lax.rem(c, 2)
            for copy in fetch(s, c, slot):
                copy.wait()

            @pl.when(c + 1 < tiles)
            def _():
                for copy in fetch(s, c + 1, 1 - slot):
                    copy.start()

            if follow is not None:
                @pl.when(c + 1 == tiles)
                def _():
                    for copy in fetch(follow, 0, 1 - slot):
                        copy.start()

            body(c, slot)
            return carry

        lax.fori_loop(0, tiles, step, 0)

    def exchange(phase, kind, block):
        def copy(p):
            target = lax.rem(e + p, experts)
            return remote(
                block(target), inbox.at[phase, kind, e],
                a2a_send.at[phase, kind, p], a2a_recv.at[phase, kind, p], (b, target),
            )
        own = pltpu.make_async_copy(block(e), inbox.at[phase, kind, e], a2a_recv.at[phase, kind, 0])

        def start():
            own.start()
            lax.fori_loop(1, experts, lambda p, carry: (copy(p).start(), carry)[1], 0)

        def wait():
            own.wait()
            lax.fori_loop(1, experts, lambda p, carry: (copy(p).wait(), carry)[1], 0)

        return start, wait


    def ring(t, j):
        if t == 0:
            source, target = token_low if j == 1 else ring_held.at[j - 1], ring_held.at[j]
        else:
            source, target = grads.at[2 - t, j - 1], grads.at[2 - t, j]
        return remote(source, target, ring_send.at[t, j], ring_recv.at[t, j], (before, e))

    def advance(t, j):
        ring(t, j - 1).wait_recv()
        ring(t, j).start()

    def far(k, p):
        target = lax.rem(e + p, experts)
        return remote(
            inbox.at[0, 0, target], far_inbox.at[k, e], far_send.at[k, p], far_recv.at[k, p], (b, target)
        )

    def far_own(k):
        return pltpu.make_async_copy(inbox.at[0, 0, e], far_inbox.at[k, e], far_recv.at[k, 0])

    def each_peer(act):
        lax.fori_loop(1, experts, lambda p, carry: (act(p), carry)[1], 0)

    def cur_load(k):
        return pltpu.make_async_copy(ring_held.at[k], cur, row_sem.at[0])

    def far_load(k):
        return pltpu.make_async_copy(far_inbox.at[k], inbox.at[0, 1], row_sem.at[1])

    def relay(k):
        if k > 1:
            each_peer(lambda p: far(k - 1, p).wait_send())
        if k == 2:
            far_own(1).wait()
        cur_load(k).wait()
        inbox[0, 0] = dot(dispatch[k], cur[...]).astype(BF).reshape(experts, slots, wide)
        far_own(k).start()
        each_peer(lambda p: far(k, p).start())

    def far_arrive(k):
        if k > 1:
            far_own(k).wait()
        each_peer(lambda p: far(k, p).wait_recv())
        far_load(k).start()

    def collect(k):
        far_load(k).wait()
        norms[1, k] = dot(packing[...], inbox[0, 1].reshape(experts * slots, wide)).astype(BF)

    def route_copy(j):
        return remote(
            routes, routes_held.at[j], route_send.at[j], route_recv.at[j],
            (lax.rem(b + groups - j, groups), e),
        )

    attention_weights = [
        pltpu.make_async_copy(w, w_held.at[i], w_sems.at[i])
        for i, w in enumerate((w_query, w_key, w_value, w_output))
    ]
    for copy in attention_weights:
        copy.start()
    normed, queries, keys, values, mixed = (attention.at[i] for i in range(5))
    normed[...] = (norm_parts(tokens[...].astype(F32))[0] * gain[...]).astype(BF)
    pl.semaphore_wait(barrier, experts + 2)
    for j in range(1, groups):
        route_copy(j).start()
    for i, result in enumerate((queries, keys, values)):
        attention_weights[i].wait()
        result[...] = dot(normed[...], w_held[i]).astype(BF)
    for copy in fetch(0, 0, 0):
        copy.start()
    allowed = allowed_pairs(ends, docs, count)
    lax.fori_loop(0, wide // 128, functools.partial(forward_pair, allowed, queries, keys, values, mixed), 0)
    attention_weights[3].wait()
    hidden[...] = tokens[...].astype(F32) + dot(mixed[...], w_held[3])
    token_low[...] = hidden[...].astype(BF)
    ring(0, 1).start()
    chosen, dispatch[0] = route_marks(routes[...], experts, slots)
    own = select_rows(chosen, cents[...], ((0,), (0,)))
    gating = jax.nn.sigmoid(jnp.sum(hidden[...] * own, axis=-1, keepdims=True))
    live = (lax.broadcasted_iota(jnp.int32, (count, 1), 0) < ends[0, docs - 1]).astype(F32)

    def out_block(kind, p):
        return outbox.at[pl.ds(pl.multiple_of((kind * experts + p) * slots, 16), slots)]

    def put_out(kind, marks, value, dims):
        start = kind * experts * slots
        outbox[start:start + experts * slots, :] = dot(marks, value, dims).astype(BF)

    send_routed, get_routed = exchange(0, 0, functools.partial(out_block, 0))
    send_grads, get_grads = exchange(0, 1, functools.partial(out_block, 1))
    send_result, get_result = exchange(1, 0, functools.partial(out_block, 0))
    send_back, get_back = exchange(1, 1, functools.partial(out_block, 1))
    put_out(0, dispatch[0], token_low[...], ((1,), (0,)))
    send_routed()
    put_out(1, dispatch[0], (gating * (live * cotangent[...].astype(F32))).astype(BF), ((1,), (0,)))
    send_grads()
    packing[...] = pack_marks(experts, slots, capacity)
    gains_out[...] = jnp.zeros_like(gains_out)
    for j in range(1, groups):
        route_copy(j).wait()
        dispatch[j] = route_marks(routes_held[j], experts, slots)[1]
    get_routed()
    stream[0] = dot(packing[...], inbox[0, 0].reshape(experts * slots, wide))
    advance(0, 2)
    cur_load(1).start()
    total = stream.at[2]

    def slab(s, c):
        return pl.ds(pl.multiple_of((s * tiles + c) * many, 16), many)

    for s in range(2):
        unit, _ = norm_parts(stream[s])
        norms[s, 0] = (unit * gain_refs[s][...]).astype(BF)
        total[...] = stream[s]

        def forward(c, slot, s=s):
            made = dot(norms[s, 0], w_held[slot])
            value, slope = gelu_pair(made)
            slopes[slab(s, c), :] = slope.astype(BF)
            total[...] += dot(value.astype(BF), w_held[2 + slot])
            if s == 1:
                @pl.when(c == tiles // 2)
                def _():
                    advance(0, 3)
                    cur_load(2).start()

        stream_tiles(s, 1, forward)
        if s == 0:
            stream[1] = total[...]
            get_grads()
            grads[1, 0] = dot(packing[...], inbox[0, 1].reshape(experts * slots, wide)).astype(BF)
            ring(1, 1).start()
            relay(1)

    put_out(0, packing[...], total[...].astype(BF), ((0,), (0,)))
    send_result()
    relay(2)
    for s in (1, 0):
        total[...] = jnp.zeros_like(total)

        def backward(c, slot, s=s):
            grad_mid = dot(grads[s, 0], w_held[2 + slot], ((1,), (1,)))
            grad_pre = (slopes[slab(s, c), :].astype(F32) * grad_mid).astype(BF)
            total[...] += dot(grad_pre, w_held[slot], ((1,), (1,)))

        stream_tiles(s, 0 if s == 1 else None, backward)
        pulled, grad_gain = norm_pull(total[...], stream[s], gain_refs[s][...])
        gains_out[pl.ds(s, 1), :] = grad_gain
        if s == 1:
            grad_stream = grads[1, 0].astype(F32) + pulled
            stream[1] = grad_stream
            grads[0, 0] = grad_stream.astype(BF)
        else:
            put_out(1, packing[...], (stream[1] + pulled).astype(BF), ((0,), (0,)))
    send_back()
    pl.semaphore_signal(ready.at[0], inc=1, device_id=to_core, device_id_type=MESH)
    for i in (3, 0, 1, 2):
        attention_weights[i].start()

    def small_step(level, peer):
        return remote(keep.at[level], s_got.at[level], small_send.at[level], small_recv.at[level], peer)

    def gain_step(level, peer):
        return remote(keep.at[5 + level, pl.ds(0, 8)], g_got.at[level], gain_send.at[level], gain_recv.at[level], peer)

    keep[5, pl.ds(0, 8)] = gains_out[...]
    gain_step(0, to_low).start()

    ring(0, 3).wait_recv()
    cur_load(3).start()
    far_arrive(1)
    collect(1)
    far_arrive(2)
    advance(1, 2)
    ring(2, 1).start()
    relay(3)
    collect(2)
    get_result()
    returned = dot(dispatch[0], inbox[1, 0].reshape(experts * slots, wide), ((0,), (0,)))
    block_out[...] = (live * (gating * returned + (1.0 - gating) * hidden[...])).astype(BF)
    grad_block = live * cotangent[...].astype(F32)
    grad_score = jnp.sum(grad_block * (returned - hidden[...]), axis=-1, keepdims=True) * gating * (1.0 - gating)
    grad_hidden = stream.at[0, pl.ds(0, count)]
    own = select_rows(chosen, cents[...], ((0,), (0,)))
    grad_hidden[...] = (1.0 - gating) * grad_block + grad_score * own
    keep[0, pl.ds(8, experts)] = select_rows(chosen, grad_score * hidden[...], ((1,), (0,)))
    turned_low = turned.at[:, pl.ds(0, count)]
    turned_low[...] = mixed[...].T
    grad_low = cur
    get_back()
    grad_hidden[...] += dot(dispatch[0], inbox[1, 1].reshape(experts * slots, wide), ((0,), (0,)))
    grad_low[...] = grad_hidden[...].astype(BF)
    attention_weights[3].wait()
    grad_mixed = dot(grad_low[...], w_held[3], ((1,), (1,))).astype(BF)
    dense_product(dense, 3, turned_low, grad_low)
    turned_low[...] = normed[...].T
    grad_low[...] = grad_mixed
    grad_three = [outbox.at[pl.ds(i * count, count)] for i in range(3)]
    lax.fori_loop(
        0, wide // 128, functools.partial(backward_pair, allowed, queries, keys, values, grad_low, grad_three), 0
    )

    def one_product(i, carry):
        dense_product(dense, i, turned_low, outbox.at[pl.ds(pl.multiple_of(i * count, 16), count)])
        return carry

    lax.fori_loop(0, 3, one_product, 0)
    for i in range(3):
        attention_weights[i].wait()
    grad_normed = sum(dot(grad_three[i][...], w_held[i], ((1,), (1,))) for i in range(3))
    pulled, grad_gain = norm_pull(grad_normed, tokens[...].astype(F32), gain[...])
    grad_tokens[...] = grad_hidden[...] + pulled
    keep[0, pl.ds(0, 8)] = jnp.broadcast_to(grad_gain, (8, wide))

    def rows_at(start, size):
        return pl.ds(pl.multiple_of(start, 32), size)

    def level_copies(level):
        copies = []
        for m in range(4):
            mine, theirs = dense.at[core, m], dense.at[other, m]
            if level == 0:
                parts = ((theirs, slopes.at[pl.ds(m * 512, 512)], to_core),)
            elif level == 1 and m < 2:
                parts = ((mine.at[rows_at((1 - x) * 256, 256)], theirs.at[pl.ds(0, 256)], to_x),)
            elif level == 1:
                parts = tuple(
                    (mine.at[rows_at(xx * 256 + (1 - y) * 128, 128)], theirs.at[pl.ds(xx * 128, 128)], to_y)
                    for xx in range(2)
                )
            elif level == 2 and m < 2:
                parts = ((mine.at[rows_at(x * 256 + (1 - y) * 128, 128)], theirs.at[pl.ds(256, 128)], to_y),)
            elif level == 2:
                parts = ((mine.at[rows_at((1 - x) * 256 + y * 128, 128)], theirs.at[pl.ds(256, 128)], to_x),)
            elif level == 3:
                start = x * 256 + y * 128 + (1 - b0) * 64
                parts = ((mine.at[rows_at(start, 64)], theirs.at[pl.ds(384, 64)], to_low),)
            else:
                start = x * 256 + y * 128 + b0 * 64 + (1 - b1) * 32
                parts = ((mine.at[rows_at(start, 32)], theirs.at[pl.ds(448, 32)], to_high),)
            for n, (src, dst, peer) in enumerate(parts):
                copies.append(remote(src, dst, dense_send.at[level, m, n], dense_recv.at[level, m, n], peer))
        return copies

    small_peers = (to_core, to_x, to_y, to_low, to_high)

    def begin(level):
        for sem in {0: (0,), 1: (1, 2), 2: (), 3: (3,), 4: (4,)}[level]:
            pl.semaphore_wait(ready.at[sem], 1)
        for copy in level_copies(level):
            copy.start()
        small_step(level, small_peers[level]).start()

    def add_rows(m, start, size, got):
        where = rows_at(start, size)
        dense[core, m, where, :] = (dense[core, m, where, :].astype(F32) + got.astype(F32)).astype(BF)

    def end(level):
        for copy in level_copies(level):
            copy.wait()
        small_step(level, small_peers[level]).wait()
        if level < 4:
            keep[level + 1] = keep[level] + s_got[level]
        for m in range(4):
            if level == 0:
                for h in range(2):
                    add_rows(m, h * 256, 256, slopes[m * 512 + h * 256:m * 512 + h * 256 + 256])
            elif level == 1 and m < 2:
                add_rows(m, x * 256, 256, dense[other, m, 0:256])
            elif level == 1:
                for xx in range(2):
                    add_rows(m, xx * 256 + y * 128, 128, dense[other, m, xx * 128:xx * 128 + 128])
            elif level == 2:
                add_rows(m, x * 256 + y * 128, 128, dense[other, m, 256:384])
            elif level == 3:
                add_rows(m, x * 256 + y * 128 + b0 * 64, 64, dense[other, m, 384:448])
            else:
                where = rows_at(x * 256 + y * 128 + b0 * 64 + b1 * 32, 32)
                dense_out[m] = dense[core, m, where, :].astype(F32) + dense[other, m, 448:480].astype(F32)
        if level == 0:
            for sem, peer in enumerate(small_peers[1:], 1):
                pl.semaphore_signal(ready.at[sem], inc=1, device_id=peer, device_id_type=MESH)
        if level == 4:
            small_out[...] = keep[4] + s_got[4]

    begin(0)
    far_arrive(3)
    advance(1, 3)
    advance(2, 2)
    collect(3)
    gain_step(0, to_low).wait()
    keep[6, pl.ds(0, 8)] = keep[5, pl.ds(0, 8)] + g_got[0]
    gain_step(1, to_high).start()
    for copy in fetch(0, 0, 0):
        copy.start()
    for k in range(1, groups):
        routed = norms[1, k].astype(F32)
        stream[k - 1] = routed
        norms[0, k] = (norm_parts(routed)[0] * gain_first[...]).astype(BF)

    def forward_others(c, slot):
        def one_group(k, carry):
            mid = gelu_pair(dot(norms[0, k + 1], w_held[slot]))[0].astype(BF)
            stream[k] += dot(mid, w_held[2 + slot])
            return carry

        lax.fori_loop(0, groups - 1, one_group, 0)

        @pl.when(c == 1)
        def _():
            end(0)
            begin(1)

    stream_tiles(0, None, forward_others)
    col = pl.multiple_of(b * width, width)
    shards = []
    for i, s in enumerate((1, 0)):
        shards.append((
            pltpu.make_async_copy(ups[s].at[0, :, pl.ds(col, width)], w_held.at[2 * i], w_sems.at[2 * i]),
            pltpu.make_async_copy(downs[s].at[0, pl.ds(col, width), :], w_held.at[2 * i + 1], w_sems.at[2 * i + 1]),
        ))
    for pair in shards:
        for copy in pair:
            copy.start()
    for k in range(1, groups):
        norms[1, k] = (norm_parts(stream[k - 1])[0] * gain_second[...]).astype(BF)
    gain_step(1, to_high).wait()
    gains_out[...] = keep[6, pl.ds(0, 8)] + g_got[1]

    quarter = wide // 4
    every = groups * many

    def down_stage(slot):
        return outbox.at[pl.ds(pl.multiple_of(slot * quarter, 16), quarter)]

    def stage_copies(s, c, slot):
        cols = pl.ds(pl.multiple_of(c * quarter, quarter), quarter)
        return (
            pltpu.make_async_copy(down_stage(slot), (down_one, down_two)[s].at[0, cols], out_sem.at[slot, 0]),
            pltpu.make_async_copy(up_stage.at[slot], (up_one, up_two)[s].at[0, :, cols], out_sem.at[slot, 1]),
        )

    chunks = width // quarter

    def weight_phase(i, carry):
        s = 1 - i

        def turn(d, carry):
            cols = pl.ds(pl.multiple_of(d * 128, 128), 128)
            turned[cols, :] = norms[s, :, :, cols].reshape(every, 128).T
            return carry

        lax.fori_loop(0, wide // 128, turn, 0)
        for n in range(2):
            @pl.when(i == n)
            def _(n=n):
                for copy in shards[n]:
                    copy.wait()
                if n == 0:
                    ring(1, 3).wait_recv()
                    advance(2, 3)
                else:
                    ring(2, 3).wait_recv()

        def chunk(c, carry):
            cols = pl.ds(pl.multiple_of(c * quarter, quarter), quarter)

            def one_group(k, carry):
                where = pl.ds(pl.multiple_of(k * many, 16), many)
                mid, slope = gelu_pair(dot(norms[s, k], w_held[2 * i, :, cols]))
                middles[0, where, :] = mid.astype(BF)
                grad_mid = dot(grads[s, k], w_held[2 * i + 1, cols, :], ((1,), (1,)))
                middles[1, where, :] = (grad_mid * slope).astype(BF)
                return carry

            lax.fori_loop(0, groups, one_group, 0)
            slot = lax.rem(c, 2)

            @pl.when(i * chunks + c > 1)
            def _():
                for copy in stage_copies(0, 0, slot):
                    copy.wait()

            down_stage(slot)[...] = dot(middles[0], grads[s].reshape(every, wide), ((0,), (0,))).astype(BF)
            up_stage[slot] = dot(turned[...], middles[1]).astype(BF)
            for n in range(2):
                @pl.when(s == n)
                def _(n=n):
                    for copy in stage_copies(n, c, slot):
                        copy.start()
            for (at_i, at_c), hook in hooks.items():
                pl.when((i == at_i) & (c == at_c))(hook)
            return carry

        lax.fori_loop(0, chunks, chunk, 0)
        return carry

    def next_level(level):
        def hook():
            end(level)
            begin(level + 1)
        return hook

    hooks = {(0, 0): next_level(1), (0, 3): next_level(2), (1, 1): next_level(3)}
    lax.fori_loop(0, 2, weight_phase, 0)
    end(4)
    for slot in range(2):
        for copy in stage_copies(0, 0, slot):
            copy.wait()
    for t in range(3):
        for j in range(1, groups):
            ring(t, j).wait_send()
    each_peer(lambda p: far(groups - 1, p).wait_send())


def dense_product(dense, which, turned, right):
    block = 32

    def one_batch(g, carry):
        rows = pl.ds(pl.multiple_of(g * 8 * block, 8 * block), 8 * block)
        product = dot(turned[rows, :], right[...]).astype(BF)
        shift = (lax.rem(g, 2) * 2 + g // 2) * block
        for e in range(8):
            place = pl.multiple_of(((e // 2) % 2 * 2 + e // 4) * 4 * block + shift, block)
            dense[e % 2, which, pl.ds(place, block)] = product[e * block:(e + 1) * block]
        return carry

    lax.fori_loop(0, 4, one_batch, 0)


def layer(
    ends, routes_row, tokens, cotangent, gain, cents, gain_first, gain_second, weights, expert_weights, slots, capacity,
):
    count, wide = tokens.shape
    experts, docs, groups = cents.shape[0], ends.shape[1], lax.axis_size("batch")
    many, ff = experts * capacity, expert_weights[0].shape[2]
    width, tiles = ff // groups, ff // wide
    vmem = pl.BlockSpec(memory_space=pltpu.VMEM)
    anys = pl.BlockSpec(memory_space=pl.ANY)
    low_out = jax.ShapeDtypeStruct((1, wide, width), BF)
    dma = pltpu.SemaphoreType.DMA
    return pl.pallas_call(
        functools.partial(layer_kernel, experts, groups, slots, capacity, docs, width, tiles),
        out_shape=(
            jax.ShapeDtypeStruct((count, wide), BF),
            jax.ShapeDtypeStruct((count, wide), F32),
            jax.ShapeDtypeStruct((4, 32, wide), F32),
            jax.ShapeDtypeStruct((8 + experts, wide), F32),
            jax.ShapeDtypeStruct((8, wide), F32),
            low_out, low_out, low_out, low_out,
            jax.ShapeDtypeStruct((groups, count, wide), BF),
            jax.ShapeDtypeStruct((groups, experts, slots, wide), BF),
        ),
        in_specs=[pl.BlockSpec(memory_space=pltpu.SMEM)] + [vmem] * 7 + [anys] * 8,
        out_specs=(vmem,) * 5 + (anys,) * 6,
        scratch_shapes=[
            pltpu.VMEM((4, wide, wide), BF),
            pltpu.VMEM((2 * tiles * many, wide), BF),
            pltpu.VMEM((3, many, wide), F32),
            pltpu.VMEM((2, groups, many, wide), BF),
            pltpu.VMEM((2, groups, many, wide), BF),
            pltpu.VMEM((count, wide), BF),
            pltpu.VMEM((count, wide), BF),
            pltpu.VMEM((5, count, wide), BF),
            pltpu.VMEM((count, wide), F32),
            pltpu.VMEM((groups, experts * slots, count), BF),
            pltpu.VMEM((many, experts * slots), BF),
            pltpu.VMEM((groups, 1, count), jnp.int32),
            pltpu.VMEM((2, 2, experts, slots, wide), BF),
            pltpu.VMEM((max(2 * experts * slots, 3 * count), wide), BF),
            pltpu.VMEM((2, 4, wide // 2, wide), BF),
            pltpu.VMEM((wide, groups * many), BF),
            pltpu.VMEM((2, groups * many, wide // 4), BF),
            pltpu.VMEM((2, wide, wide // 4), BF),
            pltpu.VMEM((7, 16, wide), F32),
            pltpu.VMEM((5, 16, wide), F32),
            pltpu.VMEM((2, 8, wide), F32),
            dma((4,)), dma((2,)), dma((2, 2, experts)), dma((2, 2, experts)), dma((groups, experts)), dma((groups, experts)),
            dma((groups,)), dma((groups,)),
            dma((3, groups)), dma((3, groups)), dma((5, 4, 2)), dma((5, 4, 2)), dma((5,)), dma((5,)),
            dma((2,)), dma((2,)), pltpu.SemaphoreType.REGULAR((5,)), dma((2, 2)),
        ],
        compiler_params=pltpu.CompilerParams(
            collective_id=1, has_side_effects=True, vmem_limit_bytes=64 * 1024 * 1024 - 65536
        ),
        name="layer",
    )(
        ends, routes_row, tokens, cotangent, gain, cents, gain_first, gain_second, *weights, *expert_weights,
    )


def hand_out_kernel(*refs):
    dense, small, gains = refs[:3]
    sources, results = refs[3:9], refs[9:]
    for i, source in enumerate(sources):
        results[i][...] = source[...].astype(results[i].dtype)

    @pl.when(pl.program_id(0) == 0)
    def _():
        for m in range(4):
            results[6 + m][...] = dense[m]
        results[10][...] = small[0:1, :]
        results[11][...] = small[8:, :]
        part = results[12].shape[1]
        where = pl.ds(pl.multiple_of(lax.axis_index("batch") * part, 128), part)
        for s in range(2):
            results[12 + s][...] = gains[s:s + 1, where]


def hand_out(dense, small, gains, *arrays):
    wide, steps = small.shape[1], 8

    def whole(shape):
        return pl.BlockSpec(shape, lambda i: (0,) * len(shape))

    def sliced(array):
        shape = array.shape[:-2] + (array.shape[-2] // steps, array.shape[-1])
        return pl.BlockSpec(shape, lambda i: (0,) * (len(shape) - 2) + (i, 0))

    shapes = [dense.shape[1:]] * 4 + [(1, wide), (small.shape[0] - 8, wide)] + [(1, wide // lax.axis_size("batch"))] * 2
    moved = [sliced(array) for array in arrays]
    return pl.pallas_call(
        hand_out_kernel,
        grid=(steps,),
        out_shape=tuple(jax.ShapeDtypeStruct(array.shape, BF if i == 4 else F32) for i, array in enumerate(arrays))
        + tuple(jax.ShapeDtypeStruct(shape, F32) for shape in shapes),
        in_specs=[whole(array.shape) for array in (dense, small, gains)] + moved,
        out_specs=tuple(moved) + tuple(whole(shape) for shape in shapes),
        compiler_params=pltpu.CompilerParams(vmem_limit_bytes=64 * 1024 * 1024 - 65536),
        name="hand_out",
    )(dense, small, gains, *arrays)


def per_device(
    tokens, doc_ends, routes, w_query, w_key, w_value, w_output, attn_gain, centroids,
    up_first, down_first, gain_first, up_second, down_second, gain_second, cotangent,
):
    count, wide = tokens.shape
    experts, groups = lax.axis_size("expert"), lax.axis_size("batch")
    capacity = 11 * count // (8 * experts)
    slots = -(-capacity // 16) * 16
    routes_row = routes.reshape(1, count)
    gain = attn_gain[None]
    weights = (w_query, w_key, w_value, w_output)
    expert_weights = (up_first, down_first, up_second, down_second)
    if groups == 4 and experts == 8:
        block_out, grad_tokens, dense, small, gains, *parts = layer(
            doc_ends, routes_row, tokens, cotangent, gain, centroids, gain_first, gain_second, weights, expert_weights,
            slots, capacity,
        )
        (
            up_one, down_one, up_two, down_two, block_out, grad_tokens, *dense, small_gain, small_cents, gain_one, gain_two,
        ) = hand_out(dense, small, gains, *parts[:4], block_out, grad_tokens)
        return (
            block_out, grad_tokens, *dense, small_gain.reshape(wide), small_cents,
            up_one, down_one, gain_one, up_two, down_two, gain_two,
        )
    *kept, out_rows = enter(doc_ends, routes_row, tokens, cotangent, gain, centroids, weights, slots)

    def exchange(blocks):
        return lax.all_to_all(blocks, "expert", split_axis=1, concat_axis=1, tiled=True)

    came = exchange(out_rows).reshape(2, experts * slots, wide)
    back, rows, gains = chain(came, *expert_weights, gain_first, gain_second, slots, capacity)
    came_back = exchange(back.reshape(out_rows.shape)).reshape(back.shape)
    block_out, grad_tokens, dense, small = leave(
        doc_ends, routes_row, tokens, cotangent, gain, centroids, kept, came_back, weights, slots
    )
    dense = scatter_sum(dense).astype(F32)
    small = all_sum(small)
    parts = []
    for s, (up, down) in enumerate(((up_first, down_first), (up_second, down_second))):
        for part in weight_grads(ring_rows(rows[0, s], "batch"), ring_rows(rows[1, s], "batch"), up[0], down[0]):
            parts.append(part[None])
    gains = jnp.sum(lax.all_gather(gains[:2], "batch"), axis=0)
    gain_part = wide // groups
    gains = lax.dynamic_slice_in_dim(gains, lax.axis_index("batch") * gain_part, gain_part, 1)
    return (
        block_out, grad_tokens, dense[0], dense[1], dense[2], dense[3], small[0], small[8:],
        parts[0], parts[1], gains[0:1], parts[2], parts[3], gains[1:2],
    )


def solution(mesh):
    return jax.shard_map(
        per_device,
        mesh=mesh,
        in_specs=(
            P(("batch", "expert"), None),
            P(("batch", "expert"), None),
            P(("batch", "expert"), None),
            P(),
            P(),
            P(),
            P(),
            P(),
            P(),
            P("expert", None, None),
            P("expert", None, None),
            P("expert", None),
            P("expert", None, None),
            P("expert", None, None),
            P("expert", None),
            P(("batch", "expert"), None),
        ),
        out_specs=(
            P(("batch", "expert"), None),
            P(("batch", "expert"), None),
            P(("batch", "expert"), None),
            P(("batch", "expert"), None),
            P(("batch", "expert"), None),
            P(("batch", "expert"), None),
            P(),
            P(),
            P("expert", None, "batch"),
            P("expert", "batch", None),
            P("expert", "batch"),
            P("expert", None, "batch"),
            P("expert", "batch", None),
            P("expert", "batch"),
        ),
        check_vma=False,
    )
```

profile of v0, /device:TPU:0, one launch (start us, length us, event | category | flops | bytes accessed | tf_op | source)
XLA Modules:
  0.0 211.0 jit_solution(5270224733553845476)
XLA Ops:
  0.7 198.5 %layer.1 = (bf16[256,1024]{1,0:T(8,128)(2,1)}, f32[256,1024]{1,0:T(8,128)}, f32[4,32,1024]{2,1,0:T(8,128)}, f32[16,1024]{1,0:T(8,128)}, f32[8,1024]{1,0:T(8,128)...) custom-call(s32[1,4]{1,0:T(1,128)} %ends.1, ...), custom_call_target="tpu_custom_call" | custom-call | tf_op jit(solution)/shard_map/layer/pallas_call | solution.py:966
  199.1 11.6 %hand_out.1 = (f32[1,1024,1024]{2,1,0:T(8,128)}, f32[1,1024,1024]{2,1,0:T(8,128)}, f32[1,1024,1024]{2,1,0:T(8,128)}, f32[1,1024,1024]{2,1,0:T(8,128)}, bf16[256,...) custom-call(f32[4,32,1024]{2,1,0:T(8,128)} %get-tuple-element.37.ref, ...), custom_call_target="tpu_custom_call" | custom-call | tf_op jit(solution)/shard_map/hand_out/pallas_call | solution.py:1046
where the time goes:
time: 211 us
  Pallas kernels  210 us (100%)
    pallas_call x1, Pallas kernels, layer(): pl.pallas_call(functools.partial(layer_kernel, experts, groups, slots, ca...  198 us
    pallas_call x1, Pallas kernels, hand_out(): pl.pallas_call(hand_out_kernel, grid=(steps,), out_shape=tuple((jax.Shape...  11.6 us

commit v1 on v0

--- a/solution.py
+++ b/solution.py
@@ -15,10 +15,9 @@
 
 def gelu_pair(v):
     square = v * v
-    bent = jnp.tanh(GELU_A * v * (1.0 + GELU_B * square))
-    half = 0.5 * (1.0 + bent)
-    slope = half + 0.5 * v * (1.0 - bent * bent) * (GELU_A * (1.0 + 3.0 * GELU_B * square))
-    return v * half, slope
+    half = 0.5 * jnp.tanh(v * (GELU_A + GELU_A * GELU_B * square)) + 0.5
+    value = v * half
+    return value, half + value * ((1.0 - half) * (2.0 * GELU_A + 6.0 * GELU_A * GELU_B * square))
 
 
 def dot(a, b, dims=((1,), (0,))):
@@ -777,7 +776,7 @@
 
     def add_rows(m, start, size, got):
         where = rows_at(start, size)
-        dense[core, m, where, :] = (dense[core, m, where, :].astype(F32) + got.astype(F32)).astype(BF)
+        dense[core, m, where, :] += got
 
     def end(level):
         for copy in level_copies(level):
@@ -890,14 +889,15 @@
             cols = pl.ds(pl.multiple_of(c * quarter, quarter), quarter)
 
             def one_group(k, carry):
-                where = pl.ds(pl.multiple_of(k * many, 16), many)
-                mid, slope = gelu_pair(dot(norms[s, k], w_held[2 * i, :, cols]))
+                where = pl.ds(pl.multiple_of(k * 2 * many, 16), 2 * many)
+                two = pl.ds(2 * k, 2)
+                mid, slope = gelu_pair(dot(norms[s, two].reshape(2 * many, wide), w_held[2 * i, :, cols]))
                 middles[0, where, :] = mid.astype(BF)
-                grad_mid = dot(grads[s, k], w_held[2 * i + 1, cols, :], ((1,), (1,)))
+                grad_mid = dot(grads[s, two].reshape(2 * many, wide), w_held[2 * i + 1, cols, :], ((1,), (1,)))
                 middles[1, where, :] = (grad_mid * slope).astype(BF)
                 return carry
 
-            lax.fori_loop(0, groups, one_group, 0)
+            lax.fori_loop(0, groups // 2, one_group, 0)
             slot = lax.rem(c, 2)
 
             @pl.when(i * chunks + c > 1)
@@ -1032,7 +1032,7 @@
 
 
 def hand_out(dense, small, gains, *arrays):
-    wide, steps = small.shape[1], 8
+    wide, steps = small.shape[1], 4
 
     def whole(shape):
         return pl.BlockSpec(shape, lambda i: (0,) * len(shape))

time: 211 us -> 208 us (0.986)
  Pallas kernels: 210 us -> 207 us
    pallas_call x1, Pallas kernels: 198 us -> 195 us  [layer(): pl.pallas_call(functools.partial(layer_kernel, experts, groups, slots, ca...]
where the time goes in v1:
time: 208 us; the launch traced here: 207 us
  Pallas kernels  207 us (100%)
    pallas_call x1, Pallas kernels, layer(): pl.pallas_call(functools.partial(layer_kernel, experts, groups, slots, ca...  195 us
    pallas_call x1, Pallas kernels, hand_out(): pl.pallas_call(hand_out_kernel, grid=(steps,), out_shape=tuple((jax.Shape...  11.3 us

profile of v1, /device:TPU:0, one launch (start us, length us, event | category | flops | bytes accessed | tf_op | source)
XLA Modules:
  0.0 207.5 jit_solution(12106892886539874755)
XLA Ops:
  0.7 195.4 %layer.1 = (bf16[256,1024]{1,0:T(8,128)(2,1)}, f32[256,1024]{1,0:T(8,128)}, f32[4,32,1024]{2,1,0:T(8,128)}, f32[16,1024]{1,0:T(8,128)}, f32[8,1024]{1,0:T(8,128)...) custom-call(s32[1,4]{1,0:T(1,128)} %ends.1, ...), custom_call_target="tpu_custom_call" | custom-call | tf_op jit(solution)/shard_map/layer/pallas_call | solution.py:966
  196.0 11.3 %hand_out.1 = (f32[1,1024,1024]{2,1,0:T(8,128)}, f32[1,1024,1024]{2,1,0:T(8,128)}, f32[1,1024,1024]{2,1,0:T(8,128)}, f32[1,1024,1024]{2,1,0:T(8,128)}, bf16[256,...) custom-call(f32[4,32,1024]{2,1,0:T(8,128)} %get-tuple-element.37.ref, ...), custom_call_target="tpu_custom_call" | custom-call | tf_op jit(solution)/shard_map/hand_out/pallas_call | solution.py:1046

commit v2 on v1

--- a/solution.py
+++ b/solution.py
@@ -581,11 +581,22 @@
     ]
     for copy in attention_weights:
         copy.start()
+    def out_block(kind, p):
+        return outbox.at[pl.ds(pl.multiple_of((kind * experts + p) * slots, 16), slots)]
+
+    def put_out(kind, marks, value, dims):
+        start = kind * experts * slots
+        outbox[start:start + experts * slots, :] = dot(marks, value, dims).astype(BF)
+
+    send_routed, get_routed = exchange(0, 0, functools.partial(out_block, 0))
+    send_grads, get_grads = exchange(0, 1, functools.partial(out_block, 1))
+    send_result, get_result = exchange(1, 0, functools.partial(out_block, 0))
+    send_back, get_back = exchange(1, 1, functools.partial(out_block, 1))
+    chosen, dispatch[0] = route_marks(routes[...], experts, slots)
+    packing[...] = pack_marks(experts, slots, capacity)
+    gains_out[...] = jnp.zeros_like(gains_out)
     normed, queries, keys, values, mixed = (attention.at[i] for i in range(5))
     normed[...] = (norm_parts(tokens[...].astype(F32))[0] * gain[...]).astype(BF)
-    pl.semaphore_wait(barrier, experts + 2)
-    for j in range(1, groups):
-        route_copy(j).start()
     for i, result in enumerate((queries, keys, values)):
         attention_weights[i].wait()
         result[...] = dot(normed[...], w_held[i]).astype(BF)
@@ -593,32 +604,21 @@
         copy.start()
     allowed = allowed_pairs(ends, docs, count)
     lax.fori_loop(0, wide // 128, functools.partial(forward_pair, allowed, queries, keys, values, mixed), 0)
+    pl.semaphore_wait(barrier, experts + 2)
+    for j in range(1, groups):
+        route_copy(j).start()
     attention_weights[3].wait()
     hidden[...] = tokens[...].astype(F32) + dot(mixed[...], w_held[3])
     token_low[...] = hidden[...].astype(BF)
+    put_out(0, dispatch[0], token_low[...], ((1,), (0,)))
+    send_routed()
     ring(0, 1).start()
-    chosen, dispatch[0] = route_marks(routes[...], experts, slots)
     own = select_rows(chosen, cents[...], ((0,), (0,)))
     gating = jax.nn.sigmoid(jnp.sum(hidden[...] * own, axis=-1, keepdims=True))
     live = (lax.broadcasted_iota(jnp.int32, (count, 1), 0) < ends[0, docs - 1]).astype(F32)
 
-    def out_block(kind, p):
-        return outbox.at[pl.ds(pl.multiple_of((kind * experts + p) * slots, 16), slots)]
-
-    def put_out(kind, marks, value, dims):
-        start = kind * experts * slots
-        outbox[start:start + experts * slots, :] = dot(marks, value, dims).astype(BF)
-
-    send_routed, get_routed = exchange(0, 0, functools.partial(out_block, 0))
-    send_grads, get_grads = exchange(0, 1, functools.partial(out_block, 1))
-    send_result, get_result = exchange(1, 0, functools.partial(out_block, 0))
-    send_back, get_back = exchange(1, 1, functools.partial(out_block, 1))
-    put_out(0, dispatch[0], token_low[...], ((1,), (0,)))
-    send_routed()
     put_out(1, dispatch[0], (gating * (live * cotangent[...].astype(F32))).astype(BF), ((1,), (0,)))
     send_grads()
-    packing[...] = pack_marks(experts, slots, capacity)
-    gains_out[...] = jnp.zeros_like(gains_out)
     for j in range(1, groups):
         route_copy(j).wait()
         dispatch[j] = route_marks(routes_held[j], experts, slots)[1]
@@ -925,7 +925,7 @@
             begin(level + 1)
         return hook
 
-    hooks = {(0, 0): next_level(1), (0, 3): next_level(2), (1, 1): next_level(3)}
+    hooks = {(0, 0): next_level(1), (0, 2): next_level(2), (1, 0): next_level(3)}
     lax.fori_loop(0, 2, weight_phase, 0)
     end(4)
     for slot in range(2):

time: 208 us -> 203 us (0.976)
  Pallas kernels: 207 us -> 201 us
    pallas_call x1, Pallas kernels: 195 us -> 190 us  [layer(): pl.pallas_call(functools.partial(layer_kernel, experts, groups, slots, ca...]
where the time goes in v2:
time: 203 us; the launch traced here: 202 us
  Pallas kernels  201 us (99%)
    pallas_call x1, Pallas kernels, layer(): pl.pallas_call(functools.partial(layer_kernel, experts, groups, slots, ca...  190 us
    pallas_call x1, Pallas kernels, hand_out(): pl.pallas_call(hand_out_kernel, grid=(steps,), out_shape=tuple((jax.Shape...  11.3 us

profile of v2, /device:TPU:0, one launch (start us, length us, event | category | flops | bytes accessed | tf_op | source)
XLA Modules:
  0.0 202.2 jit_solution(2997615737439835456)
XLA Ops:
  0.7 190.1 %layer.1 = (bf16[256,1024]{1,0:T(8,128)(2,1)}, f32[256,1024]{1,0:T(8,128)}, f32[4,32,1024]{2,1,0:T(8,128)}, f32[16,1024]{1,0:T(8,128)}, f32[8,1024]{1,0:T(8,128)...) custom-call(s32[1,4]{1,0:T(1,128)} %ends.1, ...), custom_call_target="tpu_custom_call" | custom-call | tf_op jit(solution)/shard_map/layer/pallas_call | solution.py:966
  190.8 11.3 %hand_out.1 = (f32[1,1024,1024]{2,1,0:T(8,128)}, f32[1,1024,1024]{2,1,0:T(8,128)}, f32[1,1024,1024]{2,1,0:T(8,128)}, f32[1,1024,1024]{2,1,0:T(8,128)}, bf16[256,...) custom-call(f32[4,32,1024]{2,1,0:T(8,128)} %get-tuple-element.37.ref, ...), custom_call_target="tpu_custom_call" | custom-call | tf_op jit(solution)/shard_map/hand_out/pallas_call | solution.py:1046

commit v3 on v2

--- a/solution.py
+++ b/solution.py
@@ -1032,7 +1032,7 @@
 
 
 def hand_out(dense, small, gains, *arrays):
-    wide, steps = small.shape[1], 4
+    wide, steps = small.shape[1], 2
 
     def whole(shape):
         return pl.BlockSpec(shape, lambda i: (0,) * len(shape))

time: 203 us -> 202 us (level)
  no operation moved by 1% of the time
where the time goes in v3:
time: 202 us; the launch traced here: 201 us
  Pallas kernels  200 us (99%)
    pallas_call x1, Pallas kernels, layer(): pl.pallas_call(functools.partial(layer_kernel, experts, groups, slots, ca...  190 us
    pallas_call x1, Pallas kernels, hand_out(): pl.pallas_call(hand_out_kernel, grid=(steps,), out_shape=tuple((jax.Shape...  10.3 us

profile of v3, /device:TPU:0, one launch (start us, length us, event | category | flops | bytes accessed | tf_op | source)
XLA Modules:
  0.0 201.3 jit_solution(15526888661707126746)
XLA Ops:
  0.7 190.1 %layer.1 = (bf16[256,1024]{1,0:T(8,128)(2,1)}, f32[256,1024]{1,0:T(8,128)}, f32[4,32,1024]{2,1,0:T(8,128)}, f32[16,1024]{1,0:T(8,128)}, f32[8,1024]{1,0:T(8,128)...) custom-call(s32[1,4]{1,0:T(1,128)} %ends.1, ...), custom_call_target="tpu_custom_call" | custom-call | tf_op jit(solution)/shard_map/layer/pallas_call | solution.py:966
  190.8 10.3 %hand_out.1 = (f32[1,1024,1024]{2,1,0:T(8,128)}, f32[1,1024,1024]{2,1,0:T(8,128)}, f32[1,1024,1024]{2,1,0:T(8,128)}, f32[1,1024,1024]{2,1,0:T(8,128)}, bf16[256,...) custom-call(f32[4,32,1024]{2,1,0:T(8,128)} %get-tuple-element.37.ref, ...), custom_call_target="tpu_custom_call" | custom-call | tf_op jit(solution)/shard_map/hand_out/pallas_call | solution.py:1046
